TPU v7x, 128 devices: a whole 4x4x4 slice. The times are simulated.
128 devices in a mesh: leaf: 32 (over z, y, core), rows: 4 (over x).
Axes of the slice: x: 4, y: 4, z: 4, core: 2. Of those that a mesh axis runs over, the one named last changes fastest.
Arguments:
- child_update: float32 [32, 512, 512], P('leaf', 'rows'), as said below
- block_maps: int32 [3, 32, 4], replicated, may hold values from 0 to 11, as said below
- sep_share: float32 [32, 3, 1024, 1024], P('leaf', None, 'rows'), as said below
- coupling_share: float32 [32, 3, 512, 1024], P('leaf', None, 'rows')
Outputs:
- diag_factor: float32 [32, 3, 1024, 1024], P('leaf', None, 'rows')
- below_factor: float32 [32, 3, 512, 1024], P('leaf', None, 'rows')
- top_update: float32 [32, 512, 512], P('leaf', 'rows')
Inputs may be any that keep to these rules, and one draw needn't show every extreme that they name: Each row block_maps[k, c] names 4 different front blocks; at every level k, the rows 2g and 2g+1 together name every block from 8 on. At level k only the rows c < 32 / 2^k are used. `child_update`: Symmetric. `sep_share`: symmetric in its last two dimensions.
All inputs are finite; a program needn't handle non-finite values.
Results may differ from a plain program's by a relative error of at most 0.00012.
Values sent between devices are 32-bit elements; how exact they have to be, the bound alone decides.
No kernel may reach another device: no remote copies, remote signals or barrier semaphores. Data moves between devices by JAX's collectives and lax.ppermute only.
A program may use at most 192 MiB of HBM per device.

v0:
```python
import jax
import jax.numpy as jnp
from jax import lax
from jax.sharding import PartitionSpec as P

BLK = 128
LEVELS = 3
highest = lax.Precision.HIGHEST


def partner(x, axis, stride):
    return lax.ppermute(x, axis, [(i, i ^ 1 << stride) for i in range(lax.axis_size(axis))])


def block_cholesky(matrix):
    order = matrix.shape[-1]
    if order <= 512:
        return jnp.linalg.cholesky(matrix, symmetrize_input=False)
    half = order // 2
    top_factor = block_cholesky(matrix[:half, :half])
    lower_panel = lax.linalg.triangular_solve(
        top_factor, matrix[half:, :half], left_side=False, lower=True, transpose_a=True
    )
    remainder = matrix[half:, half:] - jnp.dot(
        lower_panel, lower_panel.T, precision=highest, preferred_element_type=jnp.float32
    )
    bottom_factor = block_cholesky(remainder)
    upper_zero = jnp.zeros((half, order - half), jnp.float32)
    top_rows = jnp.concatenate([top_factor, upper_zero], axis=1)
    bottom_rows = jnp.concatenate([lower_panel, bottom_factor], axis=1)
    return jnp.concatenate([top_rows, bottom_rows], axis=0)


def sym_cholesky(matrix):
    return block_cholesky((matrix + matrix.T) * 0.5)


def place_columns(portion, block_map, blocks_front):
    count_rows = portion.shape[0]
    blocks_child = block_map.shape[0]
    selector = (block_map[None, :] == jnp.arange(blocks_front, dtype=jnp.int32)[:, None]).astype(
        jnp.float32
    )
    placed = jnp.einsum(
        "qm,nmb->nqb", selector, portion.reshape(count_rows, blocks_child, BLK), precision=highest
    )
    return placed.reshape(count_rows, blocks_front * BLK)


def pick_rows(portion, block_map, global_rows):
    count_rows = portion.shape[0]
    blocks_child = block_map.shape[0]
    matches = (block_map[None, :] == (global_rows // BLK)[:, None]).astype(jnp.int32)
    found = jnp.sum(matches, axis=1) > 0
    source_block = jnp.sum(matches * jnp.arange(blocks_child, dtype=jnp.int32)[None, :], axis=1)
    source_row = source_block * BLK + global_rows % BLK
    usable = found & (source_row >= 0) & (source_row < count_rows)
    picked = jnp.take(portion, jnp.clip(source_row, 0, count_rows - 1), axis=0)
    return jnp.where(usable[:, None], picked, 0.0)


def on_device(child_update, block_maps, sep_share, coupling_share):
    upd_rows = child_update.shape[1]
    upd_width = child_update.shape[2]
    sep_rows = sep_share.shape[2]
    sep_width = sep_share.shape[3]
    front_width = sep_width + upd_width
    blocks_front = front_width // BLK
    leaf_index = lax.axis_index("leaf")
    row_id = lax.axis_index("rows")
    targets = jnp.concatenate(
        [
            row_id * sep_rows + jnp.arange(sep_rows, dtype=jnp.int32),
            sep_width + row_id * upd_rows + jnp.arange(upd_rows, dtype=jnp.int32),
        ]
    )
    current = child_update[0]
    pend_sep = sep_share[0]
    pend_cpl = coupling_share[0]
    diag_parts = []
    below_parts = []
    for level_index in range(LEVELS):
        partner_rows, got_sep, got_cpl = partner((current, pend_sep, pend_cpl), "leaf", level_index)
        pend_sep = pend_sep + got_sep
        pend_cpl = pend_cpl + got_cpl
        sep_orig = pend_sep[0]
        cpl_orig = pend_cpl[0]
        pend_sep = pend_sep[1:]
        pend_cpl = pend_cpl[1:]
        is_right = leaf_index >> level_index & 1
        left_rows = jnp.where(is_right == 0, current, partner_rows)
        right_rows = jnp.where(is_right == 0, partner_rows, current)
        first_child = (leaf_index >> level_index + 1) * 2
        left_map = lax.dynamic_index_in_dim(block_maps[level_index], first_child, 0, keepdims=False)
        right_map = lax.dynamic_index_in_dim(
            block_maps[level_index], first_child + 1, 0, keepdims=False
        )

        def add_children(running, portions, offset, left_map=left_map, right_map=right_map):
            for portion, block_map in ((portions[0], left_map), (portions[1], right_map)):
                running = running + place_columns(
                    pick_rows(portion, block_map, targets), block_map, blocks_front
                )
            return running

        front_rows = add_children(
            jnp.zeros((sep_rows + upd_rows, front_width), jnp.float32),
            (
                lax.all_gather(left_rows, "rows", axis=0, tiled=True),
                lax.all_gather(right_rows, "rows", axis=0, tiled=True),
            ),
            jnp.int32(0),
        )
        front_pivot = front_rows[:sep_rows, :sep_width] + sep_orig
        front_below = front_rows[sep_rows:, :sep_width] + cpl_orig
        front_trail = front_rows[sep_rows:, sep_width:]
        pivot_block = lax.all_gather(front_pivot, "rows", axis=0, tiled=True)
        pivot_factor = sym_cholesky(pivot_block)
        solved = lax.linalg.triangular_solve(
            pivot_factor, front_below, left_side=False, lower=True, transpose_a=True
        )
        left_part = solved

        def product(portion, offset, left_part=left_part):
            return -jnp.dot(
                left_part, portion.T, precision=highest, preferred_element_type=jnp.float32
            )

        schur_part = front_trail + product(
            lax.all_gather(solved, "rows", axis=0, tiled=True), jnp.int32(0)
        )
        diag_parts.append(lax.dynamic_slice_in_dim(pivot_factor, row_id * sep_rows, sep_rows, 0))
        below_parts.append(solved)
        current = schur_part
    return (jnp.stack(diag_parts)[None], jnp.stack(below_parts)[None], current[None])


def solution(mesh):
    return jax.shard_map(
        on_device,
        mesh=mesh,
        in_specs=(
            P("leaf", "rows", None),
            P(),
            P("leaf", None, "rows", None),
            P("leaf", None, "rows", None),
        ),
        out_specs=(
            P("leaf", None, "rows", None),
            P("leaf", None, "rows", None),
            P("leaf", "rows", None),
        ),
        check_vma=False,
    )
```

profile of v0, /device:TPU:0, one launch (start us, length us, event | category | flops | bytes accessed | tf_op | source)
XLA Modules:
  0.0 1728.3 jit_solution(13907045781276301136)
XLA Ops:
  16.0 21.4 %all-gather.15.cloned.1.call-done = f32[512,512]{1,0:T(8,128)} async-done(((f32[128,512]{1,0:T(8,128)}), f32[512,512]{1,0:T(8,128)}) %all-gather.15.cloned.1.call-update) | async-done | bytes 1048592 | tf_op jit(solution)/shard_map/all_gather | solution.py:110
  42.0 21.4 %all-gather.13.cloned.1.call-done = f32[512,512]{1,0:T(8,128)} async-done(((f32[128,512]{1,0:T(8,128)}), f32[512,512]{1,0:T(8,128)}) %all-gather.13.cloned.1.call-update) | async-done | bytes 1048592 | tf_op jit(solution)/shard_map/all_gather | solution.py:109
  91.2 36.7 %all-gather.17.cloned.1.call-done = f32[1024,1024]{0,1:T(8,128)} async-done(((f32[256,1024]{0,1:T(8,128)}), f32[1024,1024]{0,1:T(8,128)}) %all-gather.17.cloned.1.call-update) | async-done | bytes 4194320 | tf_op jit(solution)/shard_map/all_gather | solution.py:117
  140.2 11.7 cholesky.645
  165.9 11.7 cholesky.665
  220.3 12.1 cholesky.703
  239.0 11.9 while.12
  251.6 40.1 %custom-call.48 = f32[4,128,128]{1,2,0:T(8,128)S(1)} custom-call(f32[4,128,128]{2,1,0:T(8,128)} %copy-done.32), custom_call_target="InvertDiagBlocksLowerTriangular" | custom-call | tf_op jit(solution)/shard_map/triangular_solve/custom-call.3 | solution.py:21
  340.0 12.5 cholesky.738
  372.0 13.2 cholesky.759
  426.6 28.5 %while.13 = (s32[]{:T(128)}, f32[1024,1024]{1,0:T(8,128)}, s32[8,2]{0,1:T(2,128)S(1)}, f32[8,128,128]{2,1,0:T(8,128)}, s32[]{:T(128)}) while((s32[]{:T(128)}, f32[1024,1024]{1,0:T(8,128)}, s32[8,2]{0,1:T(2,128)S(1)}, f32[8,128,128]{2,1,0:T(8,128)}, s32[]{:T(128)}) %tuple.250), condition=%wide.while_cond.1, body=%wide.while_body.1.sunk | while | flops 2 | bytes 132205 | solution.py:119
  455.0 80.2 %custom-call.52 = f32[8,128,128]{1,2,0:T(8,128)} custom-call(f32[8,128,128]{2,1,0:T(8,128)} %get-tuple-element.48), custom_call_target="InvertDiagBlocksLowerTriangular" | custom-call | tf_op jit(solution)/shard_map/triangular_solve/custom-call.8 | solution.py:119
  559.0 34.9 %all-gather.19.cloned.1.call-done = f32[512,1024]{0,1:T(8,128)} async-done(((f32[128,1024]{0,1:T(8,128)}), f32[512,1024]{0,1:T(8,128)}) %all-gather.19.cloned.1.call-update) | async-done | bytes 2097168 | tf_op jit(solution)/shard_map/all_gather | solution.py:130
  611.4 44.2 %collective-permute-done.4 = f32[2,256,1024]{1,2,0:T(8,128)} collective-permute-done((f32[2,256,1024]{1,2,0:T(8,128)}, f32[2,256,1024]{1,2,0:T(8,128)}, u32[]{:S(2)}, u32[]{:S(2)}) %collective-permute-start.4) | collective-permute-done | bytes 2097184 | tf_op jit(solution)/shard_map/ppermute | solution.py:12
  681.9 22.8 %collective-permute-done.5 = f32[2,128,1024]{1,2,0:T(8,128)S(1)} collective-permute-done((f32[2,128,1024]{1,2,0:T(8,128)}, f32[2,128,1024]{1,2,0:T(8,128)S(1)}, u32[]{:S(2)}, u32[]{:S(2)}) %collective-permute-start.5) | collective-permute-done | bytes 1048608 | tf_op jit(solution)/shard_map/ppermute | solution.py:12
  708.9 18.6 %all-gather.25.cloned.1.call-done = f32[1024,1024]{0,1:T(8,128)} async-done(((f32[256,1024]{0,1:T(8,128)}), f32[1024,1024]{0,1:T(8,128)}) %all-gather.25.cloned.1.call-update) | async-done | bytes 4194320 | tf_op jit(solution)/shard_map/all_gather | solution.py:117
  764.7 12.3 cholesky.811
  814.7 12.1 cholesky.849
  842.9 39.3 %custom-call.56 = f32[4,128,128]{1,2,0:T(8,128)S(1)} custom-call(f32[4,128,128]{2,1,0:T(8,128)S(1)} %get-tuple-element.49), custom_call_target="InvertDiagBlocksLowerTriangular" | custom-call | tf_op jit(solution)/shard_map/triangular_solve/custom-call.3 | solution.py:21
  922.7 12.5 cholesky.884
  949.9 13.2 cholesky.905
  1000.6 23.2 %while.15 = (s32[]{:T(128)}, f32[1024,1024]{1,0:T(8,128)}, s32[8,2]{0,1:T(2,128)S(1)}, f32[8,128,128]{2,1,0:T(8,128)S(1)}, s32[]{:T(128)}) while((s32[]{:T(128)}, f32[1024,1024]{1,0:T(8,128)}, s32[8,2]{0,1:T(2,128)S(1)}, f32[8,128,128]{2,1,0:T(8,128)S(1)}, s32[]{:T(128)}) %tuple.291), condition=%wide.while_cond.1.clone, body=%wide.while_body.1.clone.sunk | while | flops 2 | bytes 131189 | solution.py:119
  1023.9 79.6 %custom-call.60 = f32[8,128,128]{1,2,0:T(8,128)} custom-call(f32[8,128,128]{2,1,0:T(8,128)S(1)} %get-tuple-element.50), custom_call_target="InvertDiagBlocksLowerTriangular" | custom-call | tf_op jit(solution)/shard_map/triangular_solve/custom-call.8 | solution.py:119
  1122.9 35.0 %all-gather.27.cloned.1.call-done = f32[512,1024]{0,1:T(8,128)} async-done(((f32[128,1024]{0,1:T(8,128)}), f32[512,1024]{0,1:T(8,128)}) %all-gather.27.cloned.1.call-update) | async-done | bytes 2097168 | tf_op jit(solution)/shard_map/all_gather | solution.py:130
  1177.5 22.2 %all-gather.31.cloned.1.call-done = f32[512,512]{0,1:T(8,128)} async-done(((f32[128,512]{0,1:T(8,128)}), f32[512,512]{0,1:T(8,128)}) %all-gather.31.cloned.1.call-update) | async-done | bytes 1048592 | tf_op jit(solution)/shard_map/all_gather | solution.py:110
  1206.1 21.9 %all-gather.29.cloned.1.call-done = f32[512,512]{0,1:T(8,128)} async-done(((f32[128,512]{0,1:T(8,128)}), f32[512,512]{0,1:T(8,128)}) %all-gather.29.cloned.1.call-update) | async-done | bytes 1048592 | tf_op jit(solution)/shard_map/all_gather | solution.py:109
  1264.9 33.0 %all-gather.33.cloned.1.call-done = f32[1024,1024]{0,1:T(8,128)} async-done(((f32[256,1024]{0,1:T(8,128)}), f32[1024,1024]{0,1:T(8,128)}) %all-gather.33.cloned.1.call-update) | async-done | bytes 4194320 | tf_op jit(solution)/shard_map/all_gather | solution.py:117
  1393.4 11.9 cholesky.995
  1421.2 39.3 %custom-call.64 = f32[4,128,128]{1,2,0:T(8,128)S(1)} custom-call(f32[4,128,128]{2,1,0:T(8,128)S(1)} %get-tuple-element.51), custom_call_target="InvertDiagBlocksLowerTriangular" | custom-call | tf_op jit(solution)/shard_map/triangular_solve/custom-call.3 | solution.py:21
  1565.7 23.2 %while.17 = (s32[]{:T(128)}, f32[1024,1024]{1,0:T(8,128)}, s32[8,2]{0,1:T(2,128)S(1)}, f32[8,128,128]{2,1,0:T(8,128)S(1)}, s32[]{:T(128)}) while((s32[]{:T(128)}, f32[1024,1024]{1,0:T(8,128)}, s32[8,2]{0,1:T(2,128)S(1)}, f32[8,128,128]{2,1,0:T(8,128)S(1)}, s32[]{:T(128)}) %tuple.292), condition=%wide.while_cond.1.clone.1, body=%wide.while_body.1.clone.1.sunk | while | flops 2 | bytes 131189 | solution.py:119
  1588.9 78.8 %custom-call.68 = f32[8,128,128]{1,2,0:T(8,128)S(1)} custom-call(f32[8,128,128]{2,1,0:T(8,128)S(1)} %get-tuple-element.52), custom_call_target="InvertDiagBlocksLowerTriangular" | custom-call | tf_op jit(solution)/shard_map/triangular_solve/custom-call.8 | solution.py:119
  1692.8 22.5 %all-gather.35.cloned.1.call-done = f32[512,1024]{0,1:T(8,128)} async-done(((f32[128,1024]{0,1:T(8,128)}), f32[512,1024]{0,1:T(8,128)}) %all-gather.35.cloned.1.call-update) | async-done | bytes 2097168 | tf_op jit(solution)/shard_map/all_gather | solution.py:130
  (592 shorter events, 904.0 us)
Async XLA Ops:
  7.2 30.2 %all-gather.15.cloned.1.call-start = ((), (), s32[]{:S(2)}) async-start(), calls=%async_computation.1 | async-start | bytes 1310720 | tf_op jit(solution)/shard_map/all_gather | solution.py:110
  7.2 1.8 collective-permute-start
  10.9 52.5 %all-gather.13.cloned.1.call-start = ((), (), s32[]{:S(2)}) async-start(), calls=%async_computation | async-start | bytes 1310720 | tf_op jit(solution)/shard_map/all_gather | solution.py:109
  14.4 59.2 %collective-permute-start.1 = (f32[3,256,1024]{1,2,0:T(8,128)}, f32[3,256,1024]{1,2,0:T(8,128)}, u32[]{:S(2)}, u32[]{:S(2)}) collective-permute-start(f32[3,256,1024]{1,2,0:T(8,128)} %bitcast.5), channel_id=1, source_target_pairs={{0,4},{4,0},{8,12},{12,8},{16,20},{20,16},{24,28},{28,24},{32,36},... | collective-permute-start | bytes 9437192 | tf_op jit(solution)/shard_map/ppermute | solution.py:12
  14.6 113.3 %all-gather.17.cloned.1.call-start = ((), (), s32[]{:S(2)}) async-start(), calls=%async_computation.2 | async-start | bytes 5242880 | tf_op jit(solution)/shard_map/all_gather | solution.py:117
  79.2 514.7 %all-gather.19.cloned.1.call-start = ((), (), s32[]{:S(2)}) async-start(), calls=%async_computation.3 | async-start | bytes 2621440 | tf_op jit(solution)/shard_map/all_gather | solution.py:130
  82.3 3.8 collective-permute-start.2
  558.9 52.4 %copy-start.39 = (s32[384]{0:T(512)S(1)}, s32[384]{0:T(512)}, u32[]{:S(2)}) copy-start(s32[384]{0:T(512)} %get-tuple-element.75) | copy-start | bytes 4612
  558.9 52.4 %copy-start.40 = (s32[384]{0:T(512)S(1)}, s32[384]{0:T(512)}, u32[]{:S(2)}) copy-start(s32[384]{0:T(512)} %get-tuple-element.76) | copy-start | bytes 4612
  558.9 52.5 %copy-start.37 = (s32[384]{0:T(512)S(1)}, s32[384]{0:T(512)}, u32[]{:S(2)}) copy-start(s32[384]{0:T(512)} %get-tuple-element.73) | copy-start | bytes 4612
  558.9 52.5 %copy-start.38 = (s32[384]{0:T(512)S(1)}, s32[384]{0:T(512)}, u32[]{:S(2)}) copy-start(s32[384]{0:T(512)} %get-tuple-element.74) | copy-start | bytes 4612
  558.9 99.9 %all-gather.23.cloned.1.call-start = ((), (), s32[]{:S(2)}) async-start(), calls=%async_computation.5 | async-start | bytes 1310720 | tf_op jit(solution)/shard_map/all_gather | solution.py:110
  599.1 7.4 collective-permute-start.3
  608.3 55.4 %all-gather.21.cloned.1.call-start = ((), (), s32[]{:S(2)}) async-start(), calls=%async_computation.4 | async-start | bytes 1310720 | tf_op jit(solution)/shard_map/all_gather | solution.py:109
  609.8 45.9 %collective-permute-start.4 = (f32[2,256,1024]{1,2,0:T(8,128)}, f32[2,256,1024]{1,2,0:T(8,128)}, u32[]{:S(2)}, u32[]{:S(2)}) collective-permute-start(f32[2,256,1024]{1,2,0:T(8,128)} %slice.559), channel_id=1, source_target_pairs={{0,8},{4,12},{8,0},{12,4},{16,24},{20,28},{24,16},{28,20},{32,40},... | collective-permute-start | bytes 6291464 | tf_op jit(solution)/shard_map/ppermute | solution.py:12
  611.3 116.2 %all-gather.25.cloned.1.call-start = ((), (), s32[]{:S(2)}) async-start(), calls=%async_computation.6 | async-start | bytes 5242880 | tf_op jit(solution)/shard_map/all_gather | solution.py:117
  678.1 479.8 %all-gather.27.cloned.1.call-start = ((), (), s32[]{:S(2)}) async-start(), calls=%async_computation.7 | async-start | bytes 2621440 | tf_op jit(solution)/shard_map/all_gather | solution.py:130
  680.4 24.2 %collective-permute-start.5 = (f32[2,128,1024]{1,2,0:T(8,128)}, f32[2,128,1024]{1,2,0:T(8,128)S(1)}, u32[]{:S(2)}, u32[]{:S(2)}) collective-permute-start(f32[2,128,1024]{1,2,0:T(8,128)} %slice.576), channel_id=1, source_target_pairs={{0,8},{4,12},{8,0},{12,4},{16,24},{20,28},{24,16},{28,20},{32,40},... | collective-permute-start | bytes 3145736 | tf_op jit(solution)/shard_map/ppermute | solution.py:12
  893.3 29.3 %copy-start.17 = (f32[512,512]{1,0:T(8,128)}, f32[512,512]{1,0:T(8,128)S(1)}, u32[]{:S(2)}) copy-start(f32[512,512]{1,0:T(8,128)S(1)} %convolution_subtract_fusion.1) | copy-start | bytes 3145732
  994.0 109.5 %copy-start.22 = (f32[128,1024]{0,1:T(8,128)S(1)}, f32[128,1024]{0,1:T(8,128)}, u32[]{:S(2)}) copy-start(f32[128,1024]{0,1:T(8,128)} %fusion.50) | copy-start | bytes 1572868
  1115.5 57.8 %copy-start.35 = (s32[384]{0:T(512)S(1)}, s32[384]{0:T(512)}, u32[]{:S(2)}) copy-start(s32[384]{0:T(512)} %get-tuple-element.77) | copy-start | bytes 4612
  1115.5 57.8 %copy-start.36 = (s32[384]{0:T(512)S(1)}, s32[384]{0:T(512)}, u32[]{:S(2)}) copy-start(s32[384]{0:T(512)} %get-tuple-element.78) | copy-start | bytes 4612
  1115.5 57.9 %copy-start.33 = (s32[384]{0:T(512)S(1)}, s32[384]{0:T(512)}, u32[]{:S(2)}) copy-start(s32[384]{0:T(512)} %get-tuple-element.59) | copy-start | bytes 4612
  1115.5 57.9 %copy-start.34 = (s32[384]{0:T(512)S(1)}, s32[384]{0:T(512)}, u32[]{:S(2)}) copy-start(s32[384]{0:T(512)} %get-tuple-element.60) | copy-start | bytes 4612
  1122.9 76.8 %all-gather.31.cloned.1.call-start = ((), (), s32[]{:S(2)}) async-start(), calls=%async_computation.9 | async-start | bytes 1310720 | tf_op jit(solution)/shard_map/all_gather | solution.py:110
  1163.0 8.8 collective-permute-start.6
  1172.7 55.3 %all-gather.29.cloned.1.call-start = ((), (), s32[]{:S(2)}) async-start(), calls=%async_computation.8 | async-start | bytes 1310720 | tf_op jit(solution)/shard_map/all_gather | solution.py:109
  1173.3 124.6 %all-gather.33.cloned.1.call-start = ((), (), s32[]{:S(2)}) async-start(), calls=%async_computation.10 | async-start | bytes 5242880 | tf_op jit(solution)/shard_map/all_gather | solution.py:117
  1174.5 71.3 %collective-permute-start.7 = (f32[1,256,1024]{1,2,0:T(8,128)}, f32[1,256,1024]{1,2,0:T(8,128)}, u32[]{:S(2)}, u32[]{:S(2)}) collective-permute-start(f32[1,256,1024]{1,2,0:T(8,128)} %slice.601), channel_id=1, source_target_pairs={{0,16},{4,20},{8,24},{12,28},{16,0},{20,4},{24,8},{28,12},{32,48},... | collective-permute-start | bytes 3145736 | tf_op jit(solution)/shard_map/ppermute | solution.py:12
  1248.5 466.9 %all-gather.35.cloned.1.call-start = ((), (), s32[]{:S(2)}) async-start(), calls=%async_computation.11 | async-start | bytes 2621440 | tf_op jit(solution)/shard_map/all_gather | solution.py:130
  1248.6 14.4 collective-permute-start.8
  1560.2 107.5 %copy-start.23 = (f32[128,1024]{0,1:T(8,128)S(1)}, f32[128,1024]{0,1:T(8,128)}, u32[]{:S(2)}) copy-start(f32[128,1024]{0,1:T(8,128)} %slice_add_fusion.1) | copy-start | bytes 1572868
  (40 other events, 239.5 us)
Sparse Core Ops, SparseCore 0:
  11.0 26.3 all-gather.14
  39.1 24.2 all-gather.12
  79.4 48.5 all-gather.16
  559.0 34.8 all-gather.18
  608.4 26.8 all-gather.22
  636.8 26.8 all-gather.20
  678.3 49.1 all-gather.24
  1123.0 34.8 all-gather.26
  1172.8 26.8 all-gather.30
  1201.2 26.8 all-gather.28
  1248.7 49.1 all-gather.32
  1680.5 34.8 all-gather.34
where the time goes:
time: 1740 us; the launch traced here: 1730 us
  other arithmetic  934 us (54%)
  waiting for transfers between devices  364 us (21%)
  local copies, waits for them, and re-layouts  221 us (13%)
  matrix products  163 us (9%)
  between operations  31.4 us (2%)
    another operation x90, other arithmetic, block_cholesky(): return jnp.linalg.cholesky(matrix, symmetrize_input=False)  494 us
    another operation x5, other arithmetic, on_device(): lax.linalg.triangular_solve(pivot_factor, front_below, left_side=False, l...  245 us
    another operation x7, other arithmetic, block_cholesky(): lax.linalg.triangular_solve(top_factor, matrix[half:, :half], left_side=F...  124 us
    ppermute x9, waiting for transfers between devices, partner(): lax.ppermute(x, axis, [(i, i ^ 1 << stride) for i in range(lax.axis_size(...  94.6 us
    all_gather x3, waiting for transfers between devices, on_device(): lax.all_gather(solved, 'rows', axis=0, tiled=True)  92.4 us
    all_gather x3, waiting for transfers between devices, on_device(): pivot_block = lax.all_gather(front_pivot, 'rows', axis=0, tiled=True)  88.2 us
    another operation x76, local copies, waits for them, and re-layouts, on_device(): lax.linalg.triangular_solve(pivot_factor, front_below, left_side=False, l...  75.5 us
    another operation x45, matrix products, on_device(): lax.linalg.triangular_solve(pivot_factor, front_below, left_side=False, l...  53.7 us
  transfers between devices with their start and end apart: 21, of which 18 were waited for; matrix products, arithmetic and copies ran while one was open for 5% of the time, Pallas kernels for 0%

commit v1 on v0

--- a/solution.py
+++ b/solution.py
@@ -2,10 +2,33 @@
 import jax.numpy as jnp
 from jax import lax
 from jax.sharding import PartitionSpec as P
+from jax.lax import axis_index, axis_size, ppermute
 
 BLK = 128
 LEVELS = 3
 highest = lax.Precision.HIGHEST
+
+
+def update_row(packet, on_dim):
+    packet = jnp.moveaxis(packet, 0, on_dim)
+    v1 = packet.shape
+    return packet.reshape(*v1[:on_dim], v1[on_dim] * v1[on_dim + 1], *v1[on_dim + 2 :])
+
+
+def switch_members_all(frame, bus_axis, ndim_at):
+    lanes = axis_size(bus_axis)
+    sheets = list(map(lambda b: (b, (b + 1) % lanes), range(lanes)))
+    item_now, latest = ([], [])
+    slots = [(hop_no, dev) for dev, hop_no in sheets]
+    for k in range(lanes - 1):
+        if k % 2 == 0:
+            item_now.append(ppermute(item_now[-1] if item_now else frame, bus_axis, sheets))
+        else:
+            latest.append(ppermute(latest[-1] if latest else frame, bus_axis, slots))
+    d_next = jnp.stack([*item_now[::-1], frame, *latest], 0)
+    tile_out = axis_index(bus_axis) - len(item_now)
+    d_next = d_next[(jnp.arange(lanes) - tile_out) % lanes]
+    return update_row(d_next, ndim_at)
 
 
 def partner(x, axis, stride):
@@ -107,7 +130,7 @@
             jnp.zeros((sep_rows + upd_rows, front_width), jnp.float32),
             (
                 lax.all_gather(left_rows, "rows", axis=0, tiled=True),
-                lax.all_gather(right_rows, "rows", axis=0, tiled=True),
+                switch_members_all(right_rows, "rows", 0),
             ),
             jnp.int32(0),
         )

time: 1740 us -> 1670 us (0.960)
  waiting for transfers between devices: 364 us -> 285 us
    all_gather x3 -> x0, waiting for transfers between devices: 43.6 us -> none  [on_device(): lax.all_gather(right_rows, 'rows', axis=0, tiled=True)]
    ppermute x0 -> x9, waiting for transfers between devices: none -> 41.3 us  [the longest x6 41.3 us: switch_members_all(): ppermute(item_now[-1] if item_now else frame, bus_axis, sheets)]
    ppermute x9, waiting for transfers between devices: 94.6 us -> 56.4 us  [partner(): lax.ppermute(x, axis, [(i, i ^ 1 << stride) for i in range(lax.axis_size(...]
    all_gather x3, waiting for transfers between devices: 44.4 us -> 8.17 us  [on_device(): lax.all_gather(left_rows, 'rows', axis=0, tiled=True)]
  transfers between devices with their start and end apart: 21 -> 27, of which waited for: 18 -> 19; matrix products, arithmetic and copies ran while one was open for 5% -> 5% of each run, Pallas kernels for 0% -> 0%
where the time goes in v1:
time: 1670 us; the launch traced here: 1660 us
  other arithmetic  933 us (56%)
  waiting for transfers between devices  285 us (17%)
  local copies, waits for them, and re-layouts  222 us (13%)
  matrix products  163 us (10%)
  between operations  31.5 us (2%)
  starting transfers between devices  25.2 us (2%)
    another operation x90, other arithmetic, block_cholesky(): return jnp.linalg.cholesky(matrix, symmetrize_input=False)  494 us
    another operation x5, other arithmetic, on_device(): lax.linalg.triangular_solve(pivot_factor, front_below, left_side=False, l...  245 us
    another operation x7, other arithmetic, block_cholesky(): lax.linalg.triangular_solve(top_factor, matrix[half:, :half], left_side=F...  124 us
    all_gather x3, waiting for transfers between devices, on_device(): lax.all_gather(solved, 'rows', axis=0, tiled=True)  89.4 us
    all_gather x3, waiting for transfers between devices, on_device(): pivot_block = lax.all_gather(front_pivot, 'rows', axis=0, tiled=True)  89.3 us
    another operation x76, local copies, waits for them, and re-layouts, on_device(): lax.linalg.triangular_solve(pivot_factor, front_below, left_side=False, l...  75.5 us
    ppermute x9, waiting for transfers between devices, partner(): lax.ppermute(x, axis, [(i, i ^ 1 << stride) for i in range(lax.axis_size(...  56.4 us
    another operation x45, matrix products, on_device(): lax.linalg.triangular_solve(pivot_factor, front_below, left_side=False, l...  53.7 us
  transfers between devices with their start and end apart: 27, of which 19 were waited for; matrix products, arithmetic and copies ran while one was open for 5% of the time, Pallas kernels for 0%

profile of v1, /device:TPU:0, one launch (start us, length us, event | category | flops | bytes accessed | tf_op | source)
XLA Modules:
  0.0 1660.6 jit_solution(15116284129828641770)
XLA Ops:
  23.4 13.5 collective-permute-done.2
  68.4 38.2 %all-gather.12.cloned.1.call-done = f32[1024,1024]{0,1:T(8,128)} async-done(((f32[256,1024]{0,1:T(8,128)}), f32[1024,1024]{0,1:T(8,128)}) %all-gather.12.cloned.1.call-update) | async-done | bytes 4194320 | tf_op jit(solution)/shard_map/all_gather | solution.py:140
  118.9 11.7 cholesky.645
  144.6 11.7 cholesky.665
  173.7 11.7 cholesky.686
  198.9 12.1 cholesky.703
  217.7 11.9 while.12
  230.3 40.1 %custom-call.48 = f32[4,128,128]{1,2,0:T(8,128)S(1)} custom-call(f32[4,128,128]{2,1,0:T(8,128)} %copy-done.33), custom_call_target="InvertDiagBlocksLowerTriangular" | custom-call | tf_op jit(solution)/shard_map/triangular_solve/custom-call.3 | solution.py:44
  288.4 11.7 cholesky.718
  318.8 12.5 cholesky.738
  350.9 13.2 cholesky.759
  405.4 28.5 %while.13 = (s32[]{:T(128)}, f32[1024,1024]{1,0:T(8,128)}, s32[8,2]{0,1:T(2,128)S(1)}, f32[8,128,128]{2,1,0:T(8,128)}, s32[]{:T(128)}) while((s32[]{:T(128)}, f32[1024,1024]{1,0:T(8,128)}, s32[8,2]{0,1:T(2,128)S(1)}, f32[8,128,128]{2,1,0:T(8,128)}, s32[]{:T(128)}) %tuple.251), condition=%wide.while_cond.1, body=%wide.while_body.1.sunk | while | flops 2 | bytes 132205 | solution.py:142
  433.9 80.4 %custom-call.52 = f32[8,128,128]{1,2,0:T(8,128)} custom-call(f32[8,128,128]{2,1,0:T(8,128)} %get-tuple-element.48), custom_call_target="InvertDiagBlocksLowerTriangular" | custom-call | tf_op jit(solution)/shard_map/triangular_solve/custom-call.8 | solution.py:142
  541.0 31.9 %all-gather.14.cloned.1.call-done = f32[512,1024]{0,1:T(8,128)} async-done(((f32[128,1024]{0,1:T(8,128)}), f32[512,1024]{0,1:T(8,128)}) %all-gather.14.cloned.1.call-update) | async-done | bytes 2097168 | tf_op jit(solution)/shard_map/all_gather | solution.py:153
  579.7 13.1 collective-permute-done.6
  640.9 22.9 %collective-permute-done.11 = f32[2,128,1024]{1,2,0:T(8,128)S(1)} collective-permute-done((f32[2,128,1024]{1,2,0:T(8,128)}, f32[2,128,1024]{1,2,0:T(8,128)S(1)}, u32[]{:S(2)}, u32[]{:S(2)}) %collective-permute-start.11) | collective-permute-done | bytes 1048608 | tf_op jit(solution)/shard_map/ppermute | solution.py:35
  668.0 18.5 %all-gather.18.cloned.1.call-done = f32[1024,1024]{0,1:T(8,128)} async-done(((f32[256,1024]{0,1:T(8,128)}), f32[1024,1024]{0,1:T(8,128)}) %all-gather.18.cloned.1.call-update) | async-done | bytes 4194320 | tf_op jit(solution)/shard_map/all_gather | solution.py:140
  723.5 12.3 cholesky.811
  773.8 11.9 cholesky.849
  790.6 12.0 while.14
  802.7 39.3 %custom-call.56 = f32[4,128,128]{1,2,0:T(8,128)S(1)} custom-call(f32[4,128,128]{2,1,0:T(8,128)S(1)} %get-tuple-element.49), custom_call_target="InvertDiagBlocksLowerTriangular" | custom-call | tf_op jit(solution)/shard_map/triangular_solve/custom-call.3 | solution.py:44
  882.8 12.5 cholesky.884
  910.1 13.2 cholesky.905
  960.8 23.2 %while.15 = (s32[]{:T(128)}, f32[1024,1024]{1,0:T(8,128)}, s32[8,2]{0,1:T(2,128)S(1)}, f32[8,128,128]{2,1,0:T(8,128)S(1)}, s32[]{:T(128)}) while((s32[]{:T(128)}, f32[1024,1024]{1,0:T(8,128)}, s32[8,2]{0,1:T(2,128)S(1)}, f32[8,128,128]{2,1,0:T(8,128)S(1)}, s32[]{:T(128)}) %tuple.286), condition=%wide.while_cond.1.clone, body=%wide.while_body.1.clone.sunk | while | flops 2 | bytes 131189 | solution.py:142
  984.1 79.4 %custom-call.60 = f32[8,128,128]{1,2,0:T(8,128)} custom-call(f32[8,128,128]{2,1,0:T(8,128)S(1)} %get-tuple-element.50), custom_call_target="InvertDiagBlocksLowerTriangular" | custom-call | tf_op jit(solution)/shard_map/triangular_solve/custom-call.8 | solution.py:142
  1082.9 35.0 %all-gather.20.cloned.1.call-done = f32[512,1024]{0,1:T(8,128)} async-done(((f32[128,1024]{0,1:T(8,128)}), f32[512,1024]{0,1:T(8,128)}) %all-gather.20.cloned.1.call-update) | async-done | bytes 2097168 | tf_op jit(solution)/shard_map/all_gather | solution.py:153
  1198.0 32.7 %all-gather.24.cloned.1.call-done = f32[1024,1024]{0,1:T(8,128)} async-done(((f32[256,1024]{0,1:T(8,128)}), f32[1024,1024]{0,1:T(8,128)}) %all-gather.24.cloned.1.call-update) | async-done | bytes 4194320 | tf_op jit(solution)/shard_map/all_gather | solution.py:140
  1326.1 11.9 cholesky.995
  1353.9 39.3 %custom-call.64 = f32[4,128,128]{1,2,0:T(8,128)S(1)} custom-call(f32[4,128,128]{2,1,0:T(8,128)S(1)} %get-tuple-element.51), custom_call_target="InvertDiagBlocksLowerTriangular" | custom-call | tf_op jit(solution)/shard_map/triangular_solve/custom-call.3 | solution.py:44
  1498.4 23.2 %while.17 = (s32[]{:T(128)}, f32[1024,1024]{1,0:T(8,128)}, s32[8,2]{0,1:T(2,128)S(1)}, f32[8,128,128]{2,1,0:T(8,128)S(1)}, s32[]{:T(128)}) while((s32[]{:T(128)}, f32[1024,1024]{1,0:T(8,128)}, s32[8,2]{0,1:T(2,128)S(1)}, f32[8,128,128]{2,1,0:T(8,128)S(1)}, s32[]{:T(128)}) %tuple.287), condition=%wide.while_cond.1.clone.1, body=%wide.while_body.1.clone.1.sunk | while | flops 2 | bytes 131189 | solution.py:142
  1521.6 78.8 %custom-call.68 = f32[8,128,128]{1,2,0:T(8,128)S(1)} custom-call(f32[8,128,128]{2,1,0:T(8,128)S(1)} %get-tuple-element.52), custom_call_target="InvertDiagBlocksLowerTriangular" | custom-call | tf_op jit(solution)/shard_map/triangular_solve/custom-call.8 | solution.py:142
  1625.5 22.5 %all-gather.26.cloned.1.call-done = f32[512,1024]{0,1:T(8,128)} async-done(((f32[128,1024]{0,1:T(8,128)}), f32[512,1024]{0,1:T(8,128)}) %all-gather.26.cloned.1.call-update) | async-done | bytes 2097168 | tf_op jit(solution)/shard_map/all_gather | solution.py:153
  (615 shorter events, 908.1 us)
Async XLA Ops:
  7.2 33.4 %all-gather.10.cloned.1.call-start = ((), (), s32[]{:S(2)}) async-start(), calls=%async_computation | async-start | bytes 1310720 | tf_op jit(solution)/shard_map/all_gather | solution.py:132
  7.2 4.1 collective-permute-start
  10.9 40.0 %collective-permute-start.4 = (f32[3,256,1024]{1,2,0:T(8,128)}, f32[3,256,1024]{1,2,0:T(8,128)}, u32[]{:S(2)}, u32[]{:S(2)}) collective-permute-start(f32[3,256,1024]{1,2,0:T(8,128)} %bitcast.11), channel_id=1, source_target_pairs={{0,4},{4,0},{8,12},{12,8},{16,20},{20,16},{24,28},{28,24},{32,36},... | collective-permute-start | bytes 9437192 | tf_op jit(solution)/shard_map/ppermute | solution.py:35
  12.2 94.4 %all-gather.12.cloned.1.call-start = ((), (), s32[]{:S(2)}) async-start(), calls=%async_computation.1 | async-start | bytes 5242880 | tf_op jit(solution)/shard_map/all_gather | solution.py:140
  13.5 9.5 collective-permute-start.1
  15.2 8.2 collective-permute-start.3
  23.0 13.9 collective-permute-start.2
  56.5 516.5 %all-gather.14.cloned.1.call-start = ((), (), s32[]{:S(2)}) async-start(), calls=%async_computation.2 | async-start | bytes 2621440 | tf_op jit(solution)/shard_map/all_gather | solution.py:153
  59.5 3.8 collective-permute-start.5
  538.0 84.5 %all-gather.16.cloned.1.call-start = ((), (), s32[]{:S(2)}) async-start(), calls=%async_computation.3 | async-start | bytes 1310720 | tf_op jit(solution)/shard_map/all_gather | solution.py:132
  539.5 63.9 %collective-permute-start.10 = (f32[2,256,1024]{1,2,0:T(8,128)}, f32[2,256,1024]{1,2,0:T(8,128)}, u32[]{:S(2)}, u32[]{:S(2)}) collective-permute-start(f32[2,256,1024]{1,2,0:T(8,128)} %slice.565), channel_id=1, source_target_pairs={{0,8},{4,12},{8,0},{12,4},{16,24},{20,28},{24,16},{28,20},{32,40},... | collective-permute-start | bytes 6291464 | tf_op jit(solution)/shard_map/ppermute | solution.py:35
  578.1 14.7 collective-permute-start.6
  594.6 91.8 %all-gather.18.cloned.1.call-start = ((), (), s32[]{:S(2)}) async-start(), calls=%async_computation.4 | async-start | bytes 5242880 | tf_op jit(solution)/shard_map/all_gather | solution.py:140
  594.7 8.7 collective-permute-start.7
  595.7 11.0 collective-permute-start.9
  603.4 10.6 collective-permute-start.8
  637.1 480.8 %all-gather.20.cloned.1.call-start = ((), (), s32[]{:S(2)}) async-start(), calls=%async_computation.5 | async-start | bytes 2621440 | tf_op jit(solution)/shard_map/all_gather | solution.py:153
  639.4 24.4 %collective-permute-start.11 = (f32[2,128,1024]{1,2,0:T(8,128)}, f32[2,128,1024]{1,2,0:T(8,128)S(1)}, u32[]{:S(2)}, u32[]{:S(2)}) collective-permute-start(f32[2,128,1024]{1,2,0:T(8,128)} %slice.582), channel_id=1, source_target_pairs={{0,8},{4,12},{8,0},{12,4},{16,24},{20,28},{24,16},{28,20},{32,40},... | collective-permute-start | bytes 3145736 | tf_op jit(solution)/shard_map/ppermute | solution.py:35
  954.2 109.3 %copy-start.22 = (f32[128,1024]{0,1:T(8,128)S(1)}, f32[128,1024]{0,1:T(8,128)}, u32[]{:S(2)}) copy-start(f32[128,1024]{0,1:T(8,128)} %fusion.50) | copy-start | bytes 1572868
  1074.1 59.4 %copy-start.37 = (s32[384]{0:T(512)S(1)}, s32[384]{0:T(512)}, u32[]{:S(2)}) copy-start(s32[384]{0:T(512)} %get-tuple-element.62) | copy-start | bytes 4612
  1074.1 66.2 %copy-start.35 = (s32[384]{0:T(512)S(1)}, s32[384]{0:T(512)}, u32[]{:S(2)}) copy-start(s32[384]{0:T(512)} %get-tuple-element.80) | copy-start | bytes 4612
  1074.1 66.2 %copy-start.36 = (s32[384]{0:T(512)S(1)}, s32[384]{0:T(512)}, u32[]{:S(2)}) copy-start(s32[384]{0:T(512)} %get-tuple-element.81) | copy-start | bytes 4612
  1082.9 77.9 %all-gather.22.cloned.1.call-start = ((), (), s32[]{:S(2)}) async-start(), calls=%async_computation.6 | async-start | bytes 1310720 | tf_op jit(solution)/shard_map/all_gather | solution.py:132
  1123.1 8.8 collective-permute-start.12
  1132.6 98.1 %all-gather.24.cloned.1.call-start = ((), (), s32[]{:S(2)}) async-start(), calls=%async_computation.7 | async-start | bytes 5242880 | tf_op jit(solution)/shard_map/all_gather | solution.py:140
  1132.6 7.7 collective-permute-start.13
  1133.5 10.9 collective-permute-start.15
  1140.3 9.0 collective-permute-start.14
  1141.4 37.2 %collective-permute-start.16 = (f32[1,256,1024]{1,2,0:T(8,128)}, f32[1,256,1024]{1,2,0:T(8,128)}, u32[]{:S(2)}, u32[]{:S(2)}) collective-permute-start(f32[1,256,1024]{1,2,0:T(8,128)} %slice.607), channel_id=1, source_target_pairs={{0,16},{4,20},{8,24},{12,28},{16,0},{20,4},{24,8},{28,12},{32,48},... | collective-permute-start | bytes 3145736 | tf_op jit(solution)/shard_map/ppermute | solution.py:35
  1181.3 466.7 %all-gather.26.cloned.1.call-start = ((), (), s32[]{:S(2)}) async-start(), calls=%async_computation.8 | async-start | bytes 2621440 | tf_op jit(solution)/shard_map/all_gather | solution.py:153
  1181.4 14.7 collective-permute-start.17
  1492.9 107.5 %copy-start.23 = (f32[128,1024]{0,1:T(8,128)S(1)}, f32[128,1024]{0,1:T(8,128)}, u32[]{:S(2)}) copy-start(f32[128,1024]{0,1:T(8,128)} %slice_add_fusion.1) | copy-start | bytes 1572868
  (49 other events, 495.1 us)
Sparse Core Ops, SparseCore 0:
  12.3 28.1 all-gather.9
  56.6 49.9 all-gather.11
  538.1 34.8 all-gather.13
  594.7 27.7 all-gather.15
  637.2 49.1 all-gather.17
  1083.0 34.8 all-gather.19
  1132.7 28.0 all-gather.21
  1181.4 49.1 all-gather.23
  1613.2 34.8 all-gather.25
